TPU v7x, 32 devices: a whole 2x2x4 slice. The times are simulated.
32 devices in a mesh: heads: 2 (over core), blk: 16 (over z, y, x).
Axes of the slice: x: 2, y: 2, z: 4, core: 2. Of those that a mesh axis runs over, the one named last changes fastest.
Arguments:
- queries: bfloat16 [3072, 4096], P('blk', 'heads'), may hold values from -8 to 8
- keys: bfloat16 [3072, 4096], P('blk', 'heads'), may hold values from -6 to 6
- values: bfloat16 [3072, 4096], P('blk', 'heads'), may hold values from -24 to 24
- prefix_keys: bfloat16 [1024, 4096], P('blk', 'heads'), may hold values from -8 to 8
- prefix_values: bfloat16 [1024, 4096], P('blk', 'heads'), may hold values from -24 to 24
- lengths: int32 [24], replicated, may hold values from 1 to 224, 3072 in all
- groups: int32 [24], replicated, may hold values from 0 to 3, as said below
- out_weight: bfloat16 [4096, 4096], P('heads'), may hold values from -0.09375 to 0.09375
Outputs:
- attn_branch: bfloat16 [3072, 4096], P('blk', 'heads')
Inputs may be any that keep to these rules, and one draw needn't show every extreme that they name: Each of the 4 groups holds 6 requests. The lengths sum to 3072; the longest is 224.
All inputs are finite; a program needn't handle non-finite values.
Results may differ from a plain program's by a relative error of at most 0.019.
Values may be sent and summed in bfloat16 or wider, within the bound.
A program may use at most 128 MiB of HBM per device.

v0:
```python
import math
import jax
import jax.numpy as jnp
from jax import lax
from jax.sharding import PartitionSpec as P

HD = 128
ROT = 32
GROUPS = 4
MOST = 224


def shifted(block, axis, distance):
    devices = range(lax.axis_size(axis))
    route = [(i - distance, i) for i in devices if i - distance in devices]
    return lax.ppermute(block, axis, route)


def token_tables(lengths, groups, tok_index, prefix_len):
    ends = jnp.cumsum(lengths)
    starts = ends - lengths
    inside = (starts[None, :] <= tok_index[:, None]) & (tok_index[:, None] < ends[None, :])
    start_tok = jnp.sum(jnp.where(inside, starts[None, :] + 1, 0), axis=1) - 1
    group_tok = jnp.sum(jnp.where(inside, groups[None, :], 0), axis=1)
    position = prefix_len + tok_index - start_tok
    return (start_tok, group_tok, position)


def rotary(field, position):
    half = ROT // 2
    inverse = 10000.0 ** (-(jnp.arange(half, dtype=jnp.float32) * 2.0 / ROT))
    angle = position.astype(jnp.float32)[:, None] * inverse[None, :]
    angle = jnp.concatenate([angle, angle], axis=1)
    cosine = jnp.cos(angle)[:, None, :]
    sine = jnp.sin(angle)[:, None, :]
    front = field[..., :ROT]
    turned = jnp.concatenate([-front[..., half:], front[..., :half]], axis=-1)
    rotated = front * cosine + turned * sine
    return jnp.concatenate([rotated, field[..., ROT:]], axis=-1)


def online_update(state, q_rot, key_rows, value_rows, mask, scale):
    top_old, total_old, accum_old = state
    score = jnp.einsum("qhd,khd->hqk", q_rot, key_rows, preferred_element_type=jnp.float32) * scale
    score = jnp.where(mask[None], score, -1e30)
    top_new = jnp.maximum(top_old, jnp.max(score, axis=-1))
    expo = jnp.exp(score - top_new[..., None])
    factor = jnp.exp(top_old - top_new)
    total_new = total_old * factor + jnp.sum(expo, axis=-1)
    weights = expo.astype(jnp.bfloat16)
    accum_new = accum_old * factor[..., None] + jnp.einsum(
        "hqk,khd->hqd", weights, value_rows, preferred_element_type=jnp.float32
    )
    return (top_new, total_new, accum_new)


def body(queries, keys, values, prefix_keys, prefix_values, lengths, groups, out_weight):
    tok = queries.shape[0]
    width = queries.shape[1]
    heads_dev = width // HD
    scale = 1.0 / math.sqrt(HD)
    n_blk = lax.axis_size("blk")
    prefix_len = prefix_keys.shape[0] * n_blk // GROUPS
    first = lax.axis_index("blk") * tok
    tok_index = first + jnp.arange(tok, dtype=jnp.int32)
    start_tok, group_tok, position = token_tables(lengths, groups, tok_index, prefix_len)
    q_rot = rotary(queries.reshape(tok, heads_dev, HD).astype(jnp.float32), position).astype(
        jnp.bfloat16
    )
    k_rot = rotary(keys.reshape(tok, heads_dev, HD).astype(jnp.float32), position).astype(
        jnp.bfloat16
    )
    v_own = values.reshape(tok, heads_dev, HD)
    span = (MOST - 2) // tok + 1
    key_list = [k_rot]
    value_list = [v_own]
    index_list = [tok_index]
    for distance in range(1, span + 1):
        moved_k, moved_v = shifted((k_rot, v_own), "blk", distance)
        key_list = [moved_k] + key_list
        value_list = [moved_v] + value_list
        index_list = [tok_index - distance * tok] + index_list
    near_k = jnp.concatenate(key_list, axis=0)
    near_v = jnp.concatenate(value_list, axis=0)
    near_index = jnp.concatenate(index_list, axis=0)
    near_start = token_tables(lengths, groups, near_index, prefix_len)[0]
    near_mask = (near_start[None, :] == start_tok[:, None]) & (
        near_index[None, :] <= tok_index[:, None]
    )
    state = (
        jnp.full((heads_dev, tok), -1e30, jnp.float32),
        jnp.zeros((heads_dev, tok), jnp.float32),
        jnp.zeros((heads_dev, tok, HD), jnp.float32),
    )
    state = online_update(state, q_rot, near_k, near_v, near_mask, scale)
    piece_k = lax.all_gather(prefix_keys, "blk", axis=0, tiled=True)
    piece_v = lax.all_gather(prefix_values, "blk", axis=0, tiled=True)
    count = piece_k.shape[0]
    row_group = jnp.arange(count, dtype=jnp.int32) // prefix_len
    mask = row_group[None, :] == group_tok[:, None]
    top_final, total_final, accum_final = online_update(
        state,
        q_rot,
        piece_k.reshape(count, heads_dev, HD),
        piece_v.reshape(count, heads_dev, HD),
        mask,
        scale,
    )
    attn = accum_final / total_final[..., None]
    attn = jnp.transpose(attn, (1, 0, 2)).reshape(tok, width).astype(jnp.bfloat16)
    partial_out = jnp.dot(attn, out_weight, preferred_element_type=jnp.float32)
    projected = lax.psum_scatter(
        partial_out.astype(jnp.bfloat16), "heads", scatter_dimension=1, tiled=True
    )
    return projected


def solution(mesh):
    placed = (
        P("blk", "heads"),
        P("blk", "heads"),
        P("blk", "heads"),
        P("blk", "heads"),
        P("blk", "heads"),
        P(),
        P(),
        P("heads", None),
    )
    return jax.shard_map(
        body, mesh=mesh, in_specs=placed, out_specs=P("blk", "heads"), check_vma=False
    )
```

profile of v0, /device:TPU:0, one launch (start us, length us, event | category | flops | bytes accessed | tf_op | source)
XLA Modules:
  0.0 262.7 jit_solution(15285865329272532625)
XLA Ops:
  6.5 0.7 all-gather.3.cloned.1.call-update
  7.3 0.7 all-gather.5.cloned.1.call-update
  8.1 0.7 copy.44
  9.0 0.7 broadcast_add_fusion.2
  9.6 0.7 select_reduce_fusion.1
  10.8 0.3 fusion.70
  11.1 0.3 slice.45
  11.4 0.3 fusion.69
  11.6 1.2 slice_negate_fusion
  12.8 1.0 fusion.32
  13.8 0.4 pad_maximum_fusion.1
  14.3 4.9 %collective-permute-start = (bf16[192,16,128]{2,0,1:T(8,128)(2,1)S(1)}, bf16[192,16,128]{2,0,1:T(8,128)(2,1)S(1)}, u32[]{:S(2)}, u32[]{:S(2)}) collective-permute-start(bf16[192,16,128]{2,0,1:T(8,128)(2,1)S(1)} %pad_maximum_fusion.1), channel_id=1, source_target_pairs={{0,2},{1,3},{2,4},{3,5},{4,6},{5,7},{6,8},{7,9},{8,10},{9,11},{10,... | collective-permute-start | bytes 2359304 | tf_op jit(solution)/shard_map/ppermute | solution.py:16
  19.2 3.4 %collective-permute-start.1 = (bf16[192,16,128]{2,0,1:T(8,128)(2,1)S(1)}, bf16[192,16,128]{2,0,1:T(8,128)(2,1)S(1)}, u32[]{:S(2)}, u32[]{:S(2)}) collective-permute-start(bf16[192,16,128]{2,0,1:T(8,128)(2,1)S(1)} %pad_maximum_fusion.1), channel_id=1, source_target_pairs={{0,1},{1,2},{2,3},{3,4},{4,5},{5,6},{6,7},{7,8},{8,9},{9,10},{10,1... | collective-permute-start | bytes 2359304 | tf_op jit(solution)/shard_map/ppermute | solution.py:16
  22.7 0.2 copy_bitcast_fusion
  22.9 4.3 %collective-permute-start.2 = (bf16[192,16,128]{2,0,1:T(8,128)(2,1)S(1)}, bf16[192,16,128]{2,0,1:T(8,128)(2,1)}, u32[]{:S(2)}, u32[]{:S(2)}) collective-permute-start(bf16[192,16,128]{2,0,1:T(8,128)(2,1)S(1)} %copy_bitcast_fusion), channel_id=1, source_target_pairs={{0,2},{1,3},{2,4},{3,5},{4,6},{5,7},{6,8},{7,9},{8,10},{9,11},{10,... | collective-permute-start | bytes 2359304 | tf_op jit(solution)/shard_map/ppermute | solution.py:16
  27.1 4.3 %collective-permute-start.3 = (bf16[192,16,128]{2,0,1:T(8,128)(2,1)S(1)}, bf16[192,16,128]{2,0,1:T(8,128)(2,1)}, u32[]{:S(2)}, u32[]{:S(2)}) collective-permute-start(bf16[192,16,128]{2,0,1:T(8,128)(2,1)S(1)} %copy_bitcast_fusion), channel_id=1, source_target_pairs={{0,1},{1,2},{2,3},{3,4},{4,5},{5,6},{6,7},{7,8},{8,9},{9,10},{10,1... | collective-permute-start | bytes 2359304 | tf_op jit(solution)/shard_map/ppermute | solution.py:16
  31.4 0.3 slice.41
  31.9 0.2 compare_and_fusion
  32.1 0.2 broadcast_compare_fusion
  32.3 40.4 %collective-permute-done = bf16[192,16,128]{2,0,1:T(8,128)(2,1)S(1)} collective-permute-done((bf16[192,16,128]{2,0,1:T(8,128)(2,1)S(1)}, bf16[192,16,128]{2,0,1:T(8,128)(2,1)S(1)}, u32[]{:S(2)}, u32[]{:S(2)}) %collective-permute-start) | collective-permute-done | bytes 786464 | tf_op jit(solution)/shard_map/ppermute | solution.py:16
  72.6 4.8 %fusion.3 = (f32[16,192]{1,0:T(8,128)S(1)}, f32[16,192,576]{2,1,0:T(8,128)}) fusion(pred[192,576]{1,0:T(8,128)(4,1)S(1)} %compare_and_fusion, bf16[192,16,96]{2,0,1:T(8,128)(2,1)S(1)} %slice.45, bf16[192,16,32]{2,0,1:T(8,128)(2,1)S(1)} %get-tuple-element.19, bf16[192,16,128]{2,0,1:T(8,128)(2,1)S(1)} %collective-permute-done.1, ...), kind=kOutput, calls=%fused_computation.7 | convolution fusion | flops 469300224 | bytes 10346496 | tf_op jit(solution)/shard_map/qhd,khd->hqk/dot_general | solution.py:44
  77.5 64.7 %all-gather.3.cloned.1.call-done = bf16[1024,2048]{1,0:T(8,128)(2,1)} async-done(((bf16[64,2048]{1,0:T(8,128)(2,1)}), bf16[1024,2048]{1,0:T(8,128)(2,1)}) %all-gather.3.cloned.1.call-update) | async-done | bytes 4194320 | tf_op jit(solution)/shard_map/all_gather | solution.py:96
  142.1 6.4 %copy.54 = bf16[1024,2048]{0,1:T(8,128)(2,1)} copy(bf16[1024,2048]{1,0:T(8,128)(2,1)} %all-gather.3.cloned.1.call-done) | data formatting | bytes 8388608 | tf_op jit(solution)/shard_map/all_gather | solution.py:96
  148.6 5.2 %fusion = (f32[16,192]{1,0:T(8,128)S(1)}, f32[16,192,1024]{2,1,0:T(8,128)S(1)}) fusion(pred[192,1024]{1,0:T(8,128)(4,1)S(1)} %broadcast_compare_fusion, bf16[1024,16,128]{0,2,1:T(8,128)(2,1)} %bitcast.67, bf16[192,16,96]{2,0,1:T(8,128)(2,1)S(1)} %slice.41, bf16[192,16,32]{2,0,1:T(8,128)(2,1)S(1)} %get-tuple-element.20), kind=kOutput, calls=%fused_computation.2 | convolution fusion | flops 816313344 | bytes 17772544 | tf_op jit(solution)/shard_map/qhd,khd->hqk/dot_general | solution.py:44
  153.8 2.3 fusion.10
  156.2 3.6 %fusion.1 = f32[16,192]{1,0:T(8,128)S(1)} fusion(f32[16,192,1024]{2,1,0:T(8,128)S(1)} %get-tuple-element.31, f32[16,192]{1,0:T(8,128)S(1)} %get-tuple-element.23, pred[192,1024]{1,0:T(8,128)(4,1)S(1)} %broadcast_compare_fusion), kind=kLoop, calls=%fused_computation.3 | loop fusion | flops 12579840 | bytes 12804096 | tf_op jit(solution)/shard_map/reduce_sum | solution.py:49
  159.8 58.2 %all-gather.5.cloned.1.call-done = bf16[1024,2048]{1,0:T(8,128)(2,1)} async-done(((bf16[64,2048]{1,0:T(8,128)(2,1)}), bf16[1024,2048]{1,0:T(8,128)(2,1)}) %all-gather.5.cloned.1.call-update) | async-done | bytes 4194320 | tf_op jit(solution)/shard_map/all_gather | solution.py:97
  217.9 6.3 %copy.56 = bf16[1024,2048]{0,1:T(8,128)(2,1)} copy(bf16[1024,2048]{1,0:T(8,128)(2,1)} %all-gather.5.cloned.1.call-done) | data formatting | bytes 8388608 | tf_op jit(solution)/shard_map/all_gather | solution.py:97
  224.2 7.6 %fusion.4 = f32[16,192,128]{2,1,0:T(8,128)S(1)} fusion(bf16[1024,16,128]{0,2,1:T(8,128)(2,1)} %bitcast.70, f32[16,192,1024]{2,1,0:T(8,128)} %copy-done.2, f32[16,192]{1,0:T(8,128)S(1)} %get-tuple-element.23, pred[192,1024]{1,0:T(8,128)(4,1)S(1)} %broadcast_compare_fusion), kind=kOutput, calls=%fused_computation.8 | convolution fusion | flops 817889280 | bytes 18558976 | tf_op jit(solution)/shard_map/hqk,khd->hqd/dot_general | solution.py:51
  231.9 5.8 %fusion.42 = bf16[16,24,8,128]{3,2,1,0:T(8,128)(2,1)S(1)} fusion(f32[16,192,128]{2,1,0:T(8,128)S(1)} %fusion.4, bf16[192,16,128]{2,0,1:T(8,128)(2,1)S(1)} %copy_bitcast_fusion, bf16[192,16,128]{2,0,1:T(8,128)(2,1)} %collective-permute-done.3, bf16[192,16,128]{2,0,1:T(8,128)(2,1)} %collective-permute-done.2, f32[16,192,576]{2,1,0:T(8,128)} %get-tuple-element.29, ...), kind=kOutput, calls=%fused_computation.49 | convolution fusion | flops 469106688 | bytes 11956224 | tf_op jit(solution)/shard_map/hqk,khd->hqd/dot_general | solution.py:51
  237.7 10.6 %convolution_convert_fusion = bf16[192,4096]{1,0:T(8,128)(2,1)} fusion(bf16[2048,4096]{1,0:T(8,128)(2,1)} %param.15, bf16[16,24,8,128]{3,2,1,0:T(8,128)(2,1)S(1)} %fusion.42), kind=kOutput, calls=%fused_computation.15 | convolution fusion | flops 3222011904 | bytes 19136512 | tf_op jit(solution)/shard_map/dot_general | solution.py:111
  248.3 7.8 %reduce-scatter.2.cloned.1.call-done = bf16[192,2048]{1,0:T(8,128)(2,1)} async-done(((bf16[192,4096]{1,0:T(8,128)(2,1)}), bf16[192,2048]{1,0:T(8,128)(2,1)}) %reduce-scatter.2.cloned.1.call-update) | async-done | bytes 786448 | tf_op jit(solution)/shard_map/reduce_scatter | solution.py:112
  (38 shorter events, 0.9 us)
Async XLA Ops:
  6.5 4.2 %copy-start = (bf16[192,2048]{1,0:T(8,128)(2,1)S(1)}, bf16[192,2048]{1,0:T(8,128)(2,1)}, u32[]{:S(2)}) copy-start(bf16[192,2048]{1,0:T(8,128)(2,1)} %param.9) | copy-start | bytes 2359300
  6.5 4.8 %copy-start.4 = (bf16[192,2048]{1,0:T(8,128)(2,1)S(1)}, bf16[192,2048]{1,0:T(8,128)(2,1)}, u32[]{:S(2)}) copy-start(bf16[192,2048]{1,0:T(8,128)(2,1)} %param.8) | copy-start | bytes 2359300
  6.5 135.6 %all-gather.3.cloned.1.call-start = ((), (), s32[]{:S(2)}) async-start(), calls=%async_computation.1 | async-start | bytes 4456448 | tf_op jit(solution)/shard_map/all_gather | solution.py:96
  7.3 210.7 %all-gather.5.cloned.1.call-start = ((), (), s32[]{:S(2)}) async-start(), calls=%async_computation.2 | async-start | bytes 4456448 | tf_op jit(solution)/shard_map/all_gather | solution.py:97
  8.0 248.1 %reduce-scatter.2.cloned.1.call-start = ((), (), s32[]{:S(2)}) async-start(), calls=%async_computation.3 | async-start | bytes 2359296 | tf_op jit(solution)/shard_map/reduce_scatter | solution.py:112
  12.8 9.8 %copy-start.3 = (bf16[192,2048]{1,0:T(8,128)(2,1)S(1)}, bf16[192,2048]{1,0:T(8,128)(2,1)}, u32[]{:S(2)}) copy-start(bf16[192,2048]{1,0:T(8,128)(2,1)} %param.10) | copy-start | bytes 2359300
  14.3 58.4 %collective-permute-start = (bf16[192,16,128]{2,0,1:T(8,128)(2,1)S(1)}, bf16[192,16,128]{2,0,1:T(8,128)(2,1)S(1)}, u32[]{:S(2)}, u32[]{:S(2)}) collective-permute-start(bf16[192,16,128]{2,0,1:T(8,128)(2,1)S(1)} %pad_maximum_fusion.1), channel_id=1, source_target_pairs={{0,2},{1,3},{2,4},{3,5},{4,6},{5,7},{6,8},{7,9},{8,10},{9,11},{10,... | collective-permute-start | bytes 2359304 | tf_op jit(solution)/shard_map/ppermute | solution.py:16
  19.2 53.5 %collective-permute-start.1 = (bf16[192,16,128]{2,0,1:T(8,128)(2,1)S(1)}, bf16[192,16,128]{2,0,1:T(8,128)(2,1)S(1)}, u32[]{:S(2)}, u32[]{:S(2)}) collective-permute-start(bf16[192,16,128]{2,0,1:T(8,128)(2,1)S(1)} %pad_maximum_fusion.1), channel_id=1, source_target_pairs={{0,1},{1,2},{2,3},{3,4},{4,5},{5,6},{6,7},{7,8},{8,9},{9,10},{10,1... | collective-permute-start | bytes 2359304 | tf_op jit(solution)/shard_map/ppermute | solution.py:16
  22.9 209.0 %collective-permute-start.2 = (bf16[192,16,128]{2,0,1:T(8,128)(2,1)S(1)}, bf16[192,16,128]{2,0,1:T(8,128)(2,1)}, u32[]{:S(2)}, u32[]{:S(2)}) collective-permute-start(bf16[192,16,128]{2,0,1:T(8,128)(2,1)S(1)} %copy_bitcast_fusion), channel_id=1, source_target_pairs={{0,2},{1,3},{2,4},{3,5},{4,6},{5,7},{6,8},{7,9},{8,10},{9,11},{10,... | collective-permute-start | bytes 2359304 | tf_op jit(solution)/shard_map/ppermute | solution.py:16
  27.1 204.7 %collective-permute-start.3 = (bf16[192,16,128]{2,0,1:T(8,128)(2,1)S(1)}, bf16[192,16,128]{2,0,1:T(8,128)(2,1)}, u32[]{:S(2)}, u32[]{:S(2)}) collective-permute-start(bf16[192,16,128]{2,0,1:T(8,128)(2,1)S(1)} %copy_bitcast_fusion), channel_id=1, source_target_pairs={{0,1},{1,2},{2,3},{3,4},{4,5},{5,6},{6,7},{7,8},{8,9},{9,10},{10,1... | collective-permute-start | bytes 2359304 | tf_op jit(solution)/shard_map/ppermute | solution.py:16
  148.6 5.2 %slice-start = ((s8[7864320]{0:T(1024)(128)(4,1)}), s8[4194304]{0:T(1024)(128)(4,1)S(1)}, s32[]{:S(2)}) async-start(s8[7864320]{0:T(1024)(128)(4,1)} %bitcast.68), calls=%async_computation.4 | async-start | bytes 8388608
  148.6 5.2 %slice-start.1 = ((s8[7864320]{0:T(1024)(128)(4,1)}), s8[3670016]{0:T(1024)(128)(4,1)S(1)}, s32[]{:S(2)}) async-start(s8[7864320]{0:T(1024)(128)(4,1)} %bitcast.68), calls=%async_computation.5 | async-start | bytes 7340032
  153.8 6.0 %copy-start.2 = (f32[16,192,1024]{2,1,0:T(8,128)}, f32[16,192,1024]{2,1,0:T(8,128)S(1)}, u32[]{:S(2)}) copy-start(f32[16,192,1024]{2,1,0:T(8,128)S(1)} %get-tuple-element.31) | copy-start | bytes 37748740
  237.7 18.5 %copy-start.1 = (bf16[192,2048]{1,0:T(8,128)(2,1)S(1)}, bf16[192,2048]{1,0:T(8,128)(2,1)}, u32[]{:S(2)}) copy-start(bf16[192,2048]{1,0:T(8,128)(2,1)} %param.9) | copy-start | bytes 2359300
Sparse Core Ops, SparseCore 0:
  10.1 131.9 all-gather.2
  144.9 72.9 all-gather.4
  248.4 7.6 reduce-scatter.1
where the time goes:
time: 263 us
  waiting for transfers between devices  172 us (65%)
  matrix products  34 us (13%)
  starting transfers between devices  17 us (6%)
  local copies, waits for them, and re-layouts  14.5 us (6%)
  between operations  13.4 us (5%)
  other arithmetic  11.3 us (4%)
    all_gather x1, waiting for transfers between devices, body(): piece_k = lax.all_gather(prefix_keys, 'blk', axis=0, tiled=True)  64.7 us
    all_gather x1, waiting for transfers between devices, body(): piece_v = lax.all_gather(prefix_values, 'blk', axis=0, tiled=True)  58.2 us
    ppermute x4, waiting for transfers between devices, shifted(): return lax.ppermute(block, axis, route)  40.4 us
    ppermute x4, starting transfers between devices, shifted(): return lax.ppermute(block, axis, route)  16.9 us
    dot_general x2, matrix products, online_update(): jnp.einsum('hqk,khd->hqd', weights, value_rows, preferred_element_type=jn...  13.4 us
    dot_general x1, matrix products, body(): partial_out = jnp.dot(attn, out_weight, preferred_element_type=jnp.float32)  10.6 us
    dot_general x2, matrix products, online_update(): jnp.einsum('qhd,khd->hqk', q_rot, key_rows, preferred_element_type=jnp.fl...  9.99 us
    reduce_scatter x1, waiting for transfers between devices, body(): lax.psum_scatter(partial_out.astype(jnp.bfloat16), 'heads', scatter_dimen...  7.82 us
  transfers between devices with their start and end apart: 7, of which 4 were waited for; matrix products, arithmetic and copies ran while one was open for 17% of the time, Pallas kernels for 0%

commit v1 on v0

--- a/solution.py
+++ b/solution.py
@@ -93,7 +93,16 @@
         jnp.zeros((heads_dev, tok, HD), jnp.float32),
     )
     state = online_update(state, q_rot, near_k, near_v, near_mask, scale)
-    piece_k = lax.all_gather(prefix_keys, "blk", axis=0, tiled=True)
+    ways = lax.axis_size("blk")
+    up = [(d, (d + 1) % ways) for d in range(ways)]
+    down = [(d, (d - 1) % ways) for d in range(ways)]
+    earlier, later = ([prefix_keys], [prefix_keys])
+    for _ in range(ways // 2):
+        earlier.append(lax.ppermute(earlier[-1], "blk", up))
+    for _ in range((ways - 1) // 2):
+        later.append(lax.ppermute(later[-1], "blk", down))
+    line = jnp.concatenate([*earlier[::-1], *later[1:]], axis=0)
+    piece_k = jnp.roll(line, (lax.axis_index("blk") - ways // 2) * prefix_keys.shape[0], axis=0)
     piece_v = lax.all_gather(prefix_values, "blk", axis=0, tiled=True)
     count = piece_k.shape[0]
     row_group = jnp.arange(count, dtype=jnp.int32) // prefix_len

time: 263 us -> 355 us (1.35)
  starting transfers between devices: 17 us -> 95.4 us
  local copies, waits for them, and re-layouts: 14.5 us -> 38.4 us
  waiting for transfers between devices: 172 us -> 157 us
    ppermute x0 -> x15, waiting for transfers between devices: none -> 131 us  [the longest x8 86.2 us: body(): earlier.append(lax.ppermute(earlier[-1], 'blk', up))]
    ppermute x0 -> x15, starting transfers between devices: none -> 65.3 us  [the longest x7 46.3 us: body(): later.append(lax.ppermute(later[-1], 'blk', down))]
    all_gather x1 -> x0, waiting for transfers between devices: 64.7 us -> none  [body(): piece_k = lax.all_gather(prefix_keys, 'blk', axis=0, tiled=True)]
    all_gather x1, waiting for transfers between devices: 58.2 us -> 0.02 us  [body(): piece_v = lax.all_gather(prefix_values, 'blk', axis=0, tiled=True)]
    ppermute x4, waiting for transfers between devices: 40.4 us -> 0.01 us  [shifted(): return lax.ppermute(block, axis, route)]
    concatenate x0 -> x1, local copies, waits for them, and re-layouts: none -> 20.6 us  [body(): jnp.roll(line, (lax.axis_index('blk') - ways // 2) * prefix_keys.shape[0]...]
    reduce_scatter x1, waiting for transfers between devices: 7.82 us -> 25.5 us  [body(): lax.psum_scatter(partial_out.astype(jnp.bfloat16), 'heads', scatter_dimen...]
    ppermute x4, starting transfers between devices: 16.9 us -> 30.1 us  [shifted(): return lax.ppermute(block, axis, route)]
  transfers between devices with their start and end apart: 7 -> 21, of which waited for: 4 -> 11; matrix products, arithmetic and copies ran while one was open for 17% -> 19% of each run, Pallas kernels for 0% -> 0%
where the time goes in v1:
time: 355 us; the launch traced here: 353 us
  waiting for transfers between devices  157 us (44%)
  starting transfers between devices  95.4 us (27%)
  local copies, waits for them, and re-layouts  38.4 us (11%)
  matrix products  34.5 us (10%)
  other arithmetic  14.1 us (4%)
  between operations  13.7 us (4%)
    ppermute x8, waiting for transfers between devices, body(): earlier.append(lax.ppermute(earlier[-1], 'blk', up))  86.2 us
    ppermute x7, starting transfers between devices, body(): later.append(lax.ppermute(later[-1], 'blk', down))  46.3 us
    ppermute x7, waiting for transfers between devices, body(): later.append(lax.ppermute(later[-1], 'blk', down))  44.5 us
    ppermute x4, starting transfers between devices, shifted(): return lax.ppermute(block, axis, route)  30.1 us
    reduce_scatter x1, waiting for transfers between devices, body(): lax.psum_scatter(partial_out.astype(jnp.bfloat16), 'heads', scatter_dimen...  25.5 us
    concatenate x1, local copies, waits for them, and re-layouts, body(): jnp.roll(line, (lax.axis_index('blk') - ways // 2) * prefix_keys.shape[0]...  20.6 us
    ppermute x8, starting transfers between devices, body(): earlier.append(lax.ppermute(earlier[-1], 'blk', up))  18.9 us
    dot_general x2, matrix products, online_update(): jnp.einsum('hqk,khd->hqd', weights, value_rows, preferred_element_type=jn...  13.5 us
  transfers between devices with their start and end apart: 21, of which 11 were waited for; matrix products, arithmetic and copies ran while one was open for 19% of the time, Pallas kernels for 0%

profile of v1, /device:TPU:0, one launch (start us, length us, event | category | flops | bytes accessed | tf_op | source)
XLA Modules:
  0.0 353.0 jit_solution(1478865864723497147)
XLA Ops:
  8.5 3.0 collective-permute-start.4
  11.5 4.1 %collective-permute-start.12 = (bf16[64,2048]{0,1:T(8,128)(2,1)S(1)}, bf16[64,2048]{0,1:T(8,128)(2,1)S(1)}, u32[]{:S(2)}, u32[]{:S(2)}) collective-permute-start(bf16[64,2048]{0,1:T(8,128)(2,1)S(1)} %copy.60), channel_id=1, source_target_pairs={{0,15},{1,0},{2,1},{3,2},{4,3},{5,4},{6,5},{7,6},{8,7},{9,8},{10,9... | collective-permute-start | bytes 786440 | tf_op jit(solution)/shard_map/ppermute | solution.py:103
  20.0 15.8 %collective-permute-done.4 = bf16[64,2048]{0,1:T(8,128)(2,1)S(1)} collective-permute-done((bf16[64,2048]{0,1:T(8,128)(2,1)S(1)}, bf16[64,2048]{0,1:T(8,128)(2,1)S(1)}, u32[]{:S(2)}, u32[]{:S(2)}) %collective-permute-start.4) | collective-permute-done | bytes 262176 | tf_op jit(solution)/shard_map/ppermute | solution.py:101
  35.8 2.5 collective-permute-start.5
  39.5 3.2 collective-permute-start.13
  42.7 25.4 %collective-permute-done.5 = bf16[64,2048]{0,1:T(8,128)(2,1)S(1)} collective-permute-done((bf16[64,2048]{0,1:T(8,128)(2,1)S(1)}, bf16[64,2048]{0,1:T(8,128)(2,1)S(1)}, u32[]{:S(2)}, u32[]{:S(2)}) %collective-permute-start.5) | collective-permute-done | bytes 262176 | tf_op jit(solution)/shard_map/ppermute | solution.py:101
  68.1 2.5 collective-permute-start.6
  76.8 5.4 %collective-permute-start.1 = (bf16[192,16,128]{2,0,1:T(8,128)(2,1)}, bf16[192,16,128]{2,0,1:T(8,128)(2,1)}, u32[]{:S(2)}, u32[]{:S(2)}) collective-permute-start(bf16[192,16,128]{2,0,1:T(8,128)(2,1)} %pad_maximum_fusion.1), channel_id=1, source_target_pairs={{0,1},{1,2},{2,3},{3,4},{4,5},{5,6},{6,7},{7,8},{8,9},{9,10},{10,1... | collective-permute-start | bytes 2359304 | tf_op jit(solution)/shard_map/ppermute | solution.py:16
  83.7 3.2 collective-permute-start.7
  90.1 35.5 %collective-permute-done.14 = bf16[64,2048]{0,1:T(8,128)(2,1)S(1)} collective-permute-done((bf16[64,2048]{0,1:T(8,128)(2,1)S(1)}, bf16[64,2048]{0,1:T(8,128)(2,1)S(1)}, u32[]{:S(2)}, u32[]{:S(2)}) %collective-permute-start.14) | collective-permute-done | bytes 262176 | tf_op jit(solution)/shard_map/ppermute | solution.py:103
  125.7 18.5 %collective-permute-done.7 = bf16[64,2048]{0,1:T(8,128)(2,1)S(1)} collective-permute-done((bf16[64,2048]{0,1:T(8,128)(2,1)S(1)}, bf16[64,2048]{0,1:T(8,128)(2,1)S(1)}, u32[]{:S(2)}, u32[]{:S(2)}) %collective-permute-start.7) | collective-permute-done | bytes 262176 | tf_op jit(solution)/shard_map/ppermute | solution.py:101
  144.1 2.5 collective-permute-start.8
  146.8 5.0 %collective-permute-start.16 = (bf16[64,2048]{0,1:T(8,128)(2,1)S(1)}, bf16[64,2048]{0,1:T(8,128)(2,1)}, u32[]{:S(2)}, u32[]{:S(2)}) collective-permute-start(bf16[64,2048]{0,1:T(8,128)(2,1)S(1)} %collective-permute-done.15), channel_id=1, source_target_pairs={{0,15},{1,0},{2,1},{3,2},{4,3},{5,4},{6,5},{7,6},{8,7},{9,8},{10,9... | collective-permute-start | bytes 786440 | tf_op jit(solution)/shard_map/ppermute | solution.py:103
  151.8 11.0 %collective-permute-done.8 = bf16[64,2048]{0,1:T(8,128)(2,1)S(1)} collective-permute-done((bf16[64,2048]{0,1:T(8,128)(2,1)S(1)}, bf16[64,2048]{0,1:T(8,128)(2,1)S(1)}, u32[]{:S(2)}, u32[]{:S(2)}) %collective-permute-start.8) | collective-permute-done | bytes 262176 | tf_op jit(solution)/shard_map/ppermute | solution.py:101
  162.8 2.8 collective-permute-start.9
  165.7 5.1 %collective-permute-done.16 = bf16[64,2048]{0,1:T(8,128)(2,1)} collective-permute-done((bf16[64,2048]{0,1:T(8,128)(2,1)S(1)}, bf16[64,2048]{0,1:T(8,128)(2,1)}, u32[]{:S(2)}, u32[]{:S(2)}) %collective-permute-start.16) | collective-permute-done | bytes 262176 | tf_op jit(solution)/shard_map/ppermute | solution.py:103
  170.8 8.2 %collective-permute-done.9 = bf16[64,2048]{0,1:T(8,128)(2,1)} collective-permute-done((bf16[64,2048]{0,1:T(8,128)(2,1)S(1)}, bf16[64,2048]{0,1:T(8,128)(2,1)}, u32[]{:S(2)}, u32[]{:S(2)}) %collective-permute-start.9) | collective-permute-done | bytes 262176 | tf_op jit(solution)/shard_map/ppermute | solution.py:101
  179.0 2.6 collective-permute-start.10
  182.1 20.2 %collective-permute-start.3 = (bf16[192,16,128]{2,0,1:T(8,128)(2,1)}, bf16[192,16,128]{2,0,1:T(8,128)(2,1)}, u32[]{:S(2)}, u32[]{:S(2)}) collective-permute-start(bf16[192,16,128]{2,0,1:T(8,128)(2,1)} %copy_bitcast_fusion), channel_id=1, source_target_pairs={{0,1},{1,2},{2,3},{3,4},{4,5},{5,6},{6,7},{7,8},{8,9},{9,10},{10,1... | collective-permute-start | bytes 2359304 | tf_op jit(solution)/shard_map/ppermute | solution.py:16
  202.3 34.1 %collective-permute-start.18 = (bf16[64,2048]{0,1:T(8,128)(2,1)}, bf16[64,2048]{0,1:T(8,128)(2,1)}, u32[]{:S(2)}, u32[]{:S(2)}) collective-permute-start(bf16[64,2048]{0,1:T(8,128)(2,1)} %collective-permute-done.17), channel_id=1, source_target_pairs={{0,15},{1,0},{2,1},{3,2},{4,3},{5,4},{6,5},{7,6},{8,7},{9,8},{10,9... | collective-permute-start | bytes 786440 | tf_op jit(solution)/shard_map/ppermute | solution.py:103
  236.5 7.4 %fusion.3 = (f32[16,192]{1,0:T(8,128)S(1)}, f32[16,192,576]{2,1,0:T(8,128)}) fusion(pred[192,576]{1,0:T(8,128)(4,1)S(1)} %compare_and_fusion, bf16[192,16,96]{2,0,1:T(8,128)(2,1)S(1)} %slice.45, bf16[192,16,32]{2,0,1:T(8,128)(2,1)} %copy-done.3, bf16[192,16,128]{2,0,1:T(8,128)(2,1)} %collective-permute-done.1, ...), kind=kOutput, calls=%fused_computation.7 | convolution fusion | flops 469300224 | bytes 10346496 | tf_op jit(solution)/shard_map/qhd,khd->hqk/dot_general | solution.py:44
  243.8 3.9 %collective-permute-done.18 = bf16[64,2048]{0,1:T(8,128)(2,1)} collective-permute-done((bf16[64,2048]{0,1:T(8,128)(2,1)}, bf16[64,2048]{0,1:T(8,128)(2,1)}, u32[]{:S(2)}, u32[]{:S(2)}) %collective-permute-start.18) | collective-permute-done | bytes 262176 | tf_op jit(solution)/shard_map/ppermute | solution.py:103
  247.7 5.8 %collective-permute-done.11 = bf16[64,2048]{0,1:T(8,128)(2,1)} collective-permute-done((bf16[64,2048]{0,1:T(8,128)(2,1)}, bf16[64,2048]{0,1:T(8,128)(2,1)}, u32[]{:S(2)}, u32[]{:S(2)}) %collective-permute-start.11) | collective-permute-done | bytes 262176 | tf_op jit(solution)/shard_map/ppermute | solution.py:101
  253.5 20.6 %concatenate.49 = bf16[2048,2048]{0,1:T(8,128)(2,1)} concatenate(bf16[64,2048]{0,1:T(8,128)(2,1)} %collective-permute-done.11, bf16[64,2048]{0,1:T(8,128)(2,1)} %collective-permute-done.10, bf16[64,2048]{0,1:T(8,128)(2,1)} %collective-permute-done.9, bf16[64,2048]{0,1:T(8,128)(2,1)} %copy-done.13, bf16[64,2048]{0,1:T(8,128)(2,1)} %copy-done.11, bf16[64,2048]{0,1:T(8,128)(2,1)} %copy-done.9, ...), dimensions={0} | concatenate | bytes 16777216 | tf_op jit(solution)/shard_map/jit(_roll_dynamic)/concatenate | solution.py:105
  274.2 4.6 %constant_dynamic-slice_fusion = bf16[1024,2048]{0,1:T(8,128)(2,1)S(1)} fusion(bf16[2048,2048]{0,1:T(8,128)(2,1)} %concatenate.49, s32[]{:T(128)S(6)} %select_n.47), kind=kLoop, calls=%fused_computation.93 | loop fusion | bytes 8388612 | tf_op jit(solution)/shard_map/jit(_roll_dynamic)/dynamic_slice | solution.py:105
  278.8 3.2 fusion
  286.6 3.6 %fusion.1 = f32[16,192]{1,0:T(8,128)S(1)} fusion(f32[16,192,1024]{2,1,0:T(8,128)S(1)} %get-tuple-element.31, f32[16,192]{1,0:T(8,128)S(1)} %get-tuple-element.23, pred[192,1024]{1,0:T(8,128)(4,1)S(1)} %broadcast_compare_fusion), kind=kLoop, calls=%fused_computation.3 | loop fusion | flops 12579840 | bytes 12804096 | tf_op jit(solution)/shard_map/reduce_sum | solution.py:49
  290.2 6.4 %copy.65 = bf16[1024,2048]{0,1:T(8,128)(2,1)} copy(bf16[1024,2048]{1,0:T(8,128)(2,1)} %all-gather.2.cloned.1.call-done) | data formatting | bytes 8388608 | tf_op jit(solution)/shard_map/all_gather | solution.py:106
  296.6 7.6 %fusion.4 = f32[16,192,128]{2,1,0:T(8,128)S(1)} fusion(bf16[1024,16,128]{0,2,1:T(8,128)(2,1)} %bitcast.70, f32[16,192,1024]{2,1,0:T(8,128)} %copy-done.2, f32[16,192]{1,0:T(8,128)S(1)} %get-tuple-element.23, pred[192,1024]{1,0:T(8,128)(4,1)S(1)} %broadcast_compare_fusion), kind=kOutput, calls=%fused_computation.8 | convolution fusion | flops 817889280 | bytes 18558976 | tf_op jit(solution)/shard_map/hqk,khd->hqd/dot_general | solution.py:51
  304.3 5.9 %fusion.42 = bf16[16,24,8,128]{3,2,1,0:T(8,128)(2,1)S(1)} fusion(f32[16,192,128]{2,1,0:T(8,128)S(1)} %fusion.4, bf16[192,16,128]{2,0,1:T(8,128)(2,1)} %copy_bitcast_fusion, bf16[192,16,128]{2,0,1:T(8,128)(2,1)} %collective-permute-done.3, bf16[192,16,128]{2,0,1:T(8,128)(2,1)} %collective-permute-done.2, f32[16,192,576]{2,1,0:T(8,128)} %get-tuple-element.29, ...), kind=kOutput, calls=%fused_computation.49 | convolution fusion | flops 469106688 | bytes 11956224 | tf_op jit(solution)/shard_map/hqk,khd->hqd/dot_general | solution.py:51
  310.2 10.4 %convolution_convert_fusion = bf16[192,4096]{1,0:T(8,128)(2,1)} fusion(bf16[2048,4096]{1,0:T(8,128)(2,1)} %param.15, bf16[16,24,8,128]{3,2,1,0:T(8,128)(2,1)S(1)} %fusion.42), kind=kOutput, calls=%fused_computation.15 | convolution fusion | flops 3222011904 | bytes 19136512 | tf_op jit(solution)/shard_map/dot_general | solution.py:120
  320.7 25.5 %reduce-scatter.2.cloned.1.call-done = bf16[192,2048]{1,0:T(8,128)(2,1)} async-done(((bf16[192,4096]{1,0:T(8,128)(2,1)}), bf16[192,2048]{1,0:T(8,128)(2,1)}) %reduce-scatter.2.cloned.1.call-update) | async-done | bytes 786448 | tf_op jit(solution)/shard_map/reduce_scatter | solution.py:121
  (87 shorter events, 23.9 us)
Async XLA Ops:
  6.5 11.8 %copy-start = (bf16[192,2048]{1,0:T(8,128)(2,1)S(1)}, bf16[192,2048]{1,0:T(8,128)(2,1)}, u32[]{:S(2)}) copy-start(bf16[192,2048]{1,0:T(8,128)(2,1)} %param.9) | copy-start | bytes 2359300
  6.5 283.7 %all-gather.2.cloned.1.call-start = ((), (), s32[]{:S(2)}) async-start(), calls=%async_computation.1 | async-start | bytes 4456448 | tf_op jit(solution)/shard_map/all_gather | solution.py:106
  7.3 338.9 %reduce-scatter.2.cloned.1.call-start = ((), (), s32[]{:S(2)}) async-start(), calls=%async_computation.2 | async-start | bytes 2359296 | tf_op jit(solution)/shard_map/reduce_scatter | solution.py:121
  8.5 27.3 %collective-permute-start.4 = (bf16[64,2048]{0,1:T(8,128)(2,1)S(1)}, bf16[64,2048]{0,1:T(8,128)(2,1)S(1)}, u32[]{:S(2)}, u32[]{:S(2)}) collective-permute-start(bf16[64,2048]{0,1:T(8,128)(2,1)S(1)} %copy.60), channel_id=1, source_target_pairs={{0,1},{1,2},{2,3},{3,4},{4,5},{5,6},{6,7},{7,8},{8,9},{9,10},{10,1... | collective-permute-start | bytes 786440 | tf_op jit(solution)/shard_map/ppermute | solution.py:101
  11.5 27.9 %collective-permute-start.12 = (bf16[64,2048]{0,1:T(8,128)(2,1)S(1)}, bf16[64,2048]{0,1:T(8,128)(2,1)S(1)}, u32[]{:S(2)}, u32[]{:S(2)}) collective-permute-start(bf16[64,2048]{0,1:T(8,128)(2,1)S(1)} %copy.60), channel_id=1, source_target_pairs={{0,15},{1,0},{2,1},{3,2},{4,3},{5,4},{6,5},{7,6},{8,7},{9,8},{10,9... | collective-permute-start | bytes 786440 | tf_op jit(solution)/shard_map/ppermute | solution.py:103
  35.8 32.3 %collective-permute-start.5 = (bf16[64,2048]{0,1:T(8,128)(2,1)S(1)}, bf16[64,2048]{0,1:T(8,128)(2,1)S(1)}, u32[]{:S(2)}, u32[]{:S(2)}) collective-permute-start(bf16[64,2048]{0,1:T(8,128)(2,1)S(1)} %collective-permute-done.4), channel_id=1, source_target_pairs={{0,1},{1,2},{2,3},{3,4},{4,5},{5,6},{6,7},{7,8},{8,9},{9,10},{10,1... | collective-permute-start | bytes 786440 | tf_op jit(solution)/shard_map/ppermute | solution.py:101
  39.5 32.9 %copy-start.5 = (bf16[64,2048]{0,1:T(8,128)(2,1)}, bf16[64,2048]{0,1:T(8,128)(2,1)S(1)}, u32[]{:S(2)}) copy-start(bf16[64,2048]{0,1:T(8,128)(2,1)S(1)} %collective-permute-done.12) | copy-start | bytes 786436
  39.5 42.7 %collective-permute-start.13 = (bf16[64,2048]{0,1:T(8,128)(2,1)S(1)}, bf16[64,2048]{0,1:T(8,128)(2,1)S(1)}, u32[]{:S(2)}, u32[]{:S(2)}) collective-permute-start(bf16[64,2048]{0,1:T(8,128)(2,1)S(1)} %collective-permute-done.12), channel_id=1, source_target_pairs={{0,15},{1,0},{2,1},{3,2},{4,3},{5,4},{6,5},{7,6},{8,7},{9,8},{10,9... | collective-permute-start | bytes 786440 | tf_op jit(solution)/shard_map/ppermute | solution.py:103
  68.1 15.5 %collective-permute-start.6 = (bf16[64,2048]{0,1:T(8,128)(2,1)S(1)}, bf16[64,2048]{0,1:T(8,128)(2,1)S(1)}, u32[]{:S(2)}, u32[]{:S(2)}) collective-permute-start(bf16[64,2048]{0,1:T(8,128)(2,1)S(1)} %collective-permute-done.5), channel_id=1, source_target_pairs={{0,1},{1,2},{2,3},{3,4},{4,5},{5,6},{6,7},{7,8},{8,9},{9,10},{10,1... | collective-permute-start | bytes 786440 | tf_op jit(solution)/shard_map/ppermute | solution.py:101
  72.4 14.4 %copy-start.14 = (bf16[192,2048]{1,0:T(8,128)(2,1)S(1)}, bf16[192,2048]{1,0:T(8,128)(2,1)}, u32[]{:S(2)}) copy-start(bf16[192,2048]{1,0:T(8,128)(2,1)} %param.10) | copy-start | bytes 2359300
  74.6 107.5 %collective-permute-start = (bf16[192,16,128]{2,0,1:T(8,128)(2,1)}, bf16[192,16,128]{2,0,1:T(8,128)(2,1)}, u32[]{:S(2)}, u32[]{:S(2)}) collective-permute-start(bf16[192,16,128]{2,0,1:T(8,128)(2,1)} %pad_maximum_fusion.1), channel_id=1, source_target_pairs={{0,2},{1,3},{2,4},{3,5},{4,6},{5,7},{6,8},{7,9},{8,10},{9,11},{10,... | collective-permute-start | bytes 2359304 | tf_op jit(solution)/shard_map/ppermute | solution.py:16
  76.8 159.7 %collective-permute-start.1 = (bf16[192,16,128]{2,0,1:T(8,128)(2,1)}, bf16[192,16,128]{2,0,1:T(8,128)(2,1)}, u32[]{:S(2)}, u32[]{:S(2)}) collective-permute-start(bf16[192,16,128]{2,0,1:T(8,128)(2,1)} %pad_maximum_fusion.1), channel_id=1, source_target_pairs={{0,1},{1,2},{2,3},{3,4},{4,5},{5,6},{6,7},{7,8},{8,9},{9,10},{10,1... | collective-permute-start | bytes 2359304 | tf_op jit(solution)/shard_map/ppermute | solution.py:16
  82.2 43.4 %collective-permute-start.14 = (bf16[64,2048]{0,1:T(8,128)(2,1)S(1)}, bf16[64,2048]{0,1:T(8,128)(2,1)S(1)}, u32[]{:S(2)}, u32[]{:S(2)}) collective-permute-start(bf16[64,2048]{0,1:T(8,128)(2,1)S(1)} %collective-permute-done.13), channel_id=1, source_target_pairs={{0,15},{1,0},{2,1},{3,2},{4,3},{5,4},{6,5},{7,6},{8,7},{9,8},{10,9... | collective-permute-start | bytes 786440 | tf_op jit(solution)/shard_map/ppermute | solution.py:103
  83.6 42.0 %copy-start.9 = (bf16[64,2048]{0,1:T(8,128)(2,1)}, bf16[64,2048]{0,1:T(8,128)(2,1)S(1)}, u32[]{:S(2)}) copy-start(bf16[64,2048]{0,1:T(8,128)(2,1)S(1)} %collective-permute-done.6) | copy-start | bytes 786436
  83.7 60.5 %collective-permute-start.7 = (bf16[64,2048]{0,1:T(8,128)(2,1)S(1)}, bf16[64,2048]{0,1:T(8,128)(2,1)S(1)}, u32[]{:S(2)}, u32[]{:S(2)}) collective-permute-start(bf16[64,2048]{0,1:T(8,128)(2,1)S(1)} %collective-permute-done.6), channel_id=1, source_target_pairs={{0,1},{1,2},{2,3},{3,4},{4,5},{5,6},{6,7},{7,8},{8,9},{9,10},{10,1... | collective-permute-start | bytes 786440 | tf_op jit(solution)/shard_map/ppermute | solution.py:101
  87.9 216.3 %collective-permute-start.2 = (bf16[192,16,128]{2,0,1:T(8,128)(2,1)}, bf16[192,16,128]{2,0,1:T(8,128)(2,1)}, u32[]{:S(2)}, u32[]{:S(2)}) collective-permute-start(bf16[192,16,128]{2,0,1:T(8,128)(2,1)} %copy_bitcast_fusion), channel_id=1, source_target_pairs={{0,2},{1,3},{2,4},{3,5},{4,6},{5,7},{6,8},{7,9},{8,10},{9,11},{10,... | collective-permute-start | bytes 2359304 | tf_op jit(solution)/shard_map/ppermute | solution.py:16
  125.7 55.9 %copy-start.10 = (bf16[64,2048]{0,1:T(8,128)(2,1)}, bf16[64,2048]{0,1:T(8,128)(2,1)S(1)}, u32[]{:S(2)}) copy-start(bf16[64,2048]{0,1:T(8,128)(2,1)S(1)} %collective-permute-done.14) | copy-start | bytes 786436
  125.7 21.1 %collective-permute-start.15 = (bf16[64,2048]{0,1:T(8,128)(2,1)S(1)}, bf16[64,2048]{0,1:T(8,128)(2,1)S(1)}, u32[]{:S(2)}, u32[]{:S(2)}) collective-permute-start(bf16[64,2048]{0,1:T(8,128)(2,1)S(1)} %collective-permute-done.14), channel_id=1, source_target_pairs={{0,15},{1,0},{2,1},{3,2},{4,3},{5,4},{6,5},{7,6},{8,7},{9,8},{10,9... | collective-permute-start | bytes 786440 | tf_op jit(solution)/shard_map/ppermute | solution.py:103
  144.1 18.6 %collective-permute-start.8 = (bf16[64,2048]{0,1:T(8,128)(2,1)S(1)}, bf16[64,2048]{0,1:T(8,128)(2,1)S(1)}, u32[]{:S(2)}, u32[]{:S(2)}) collective-permute-start(bf16[64,2048]{0,1:T(8,128)(2,1)S(1)} %collective-permute-done.7), channel_id=1, source_target_pairs={{0,1},{1,2},{2,3},{3,4},{4,5},{5,6},{6,7},{7,8},{8,9},{9,10},{10,1... | collective-permute-start | bytes 786440 | tf_op jit(solution)/shard_map/ppermute | solution.py:101
  146.8 16.0 %copy-start.12 = (bf16[64,2048]{0,1:T(8,128)(2,1)}, bf16[64,2048]{0,1:T(8,128)(2,1)S(1)}, u32[]{:S(2)}) copy-start(bf16[64,2048]{0,1:T(8,128)(2,1)S(1)} %collective-permute-done.15) | copy-start | bytes 786436
  146.8 24.0 %collective-permute-start.16 = (bf16[64,2048]{0,1:T(8,128)(2,1)S(1)}, bf16[64,2048]{0,1:T(8,128)(2,1)}, u32[]{:S(2)}, u32[]{:S(2)}) collective-permute-start(bf16[64,2048]{0,1:T(8,128)(2,1)S(1)} %collective-permute-done.15), channel_id=1, source_target_pairs={{0,15},{1,0},{2,1},{3,2},{4,3},{5,4},{6,5},{7,6},{8,7},{9,8},{10,9... | collective-permute-start | bytes 786440 | tf_op jit(solution)/shard_map/ppermute | solution.py:103
  162.8 8.0 %copy-start.13 = (bf16[64,2048]{0,1:T(8,128)(2,1)}, bf16[64,2048]{0,1:T(8,128)(2,1)S(1)}, u32[]{:S(2)}) copy-start(bf16[64,2048]{0,1:T(8,128)(2,1)S(1)} %collective-permute-done.8) | copy-start | bytes 786436
  162.8 16.2 %collective-permute-start.9 = (bf16[64,2048]{0,1:T(8,128)(2,1)S(1)}, bf16[64,2048]{0,1:T(8,128)(2,1)}, u32[]{:S(2)}, u32[]{:S(2)}) collective-permute-start(bf16[64,2048]{0,1:T(8,128)(2,1)S(1)} %collective-permute-done.8), channel_id=1, source_target_pairs={{0,1},{1,2},{2,3},{3,4},{4,5},{5,6},{6,7},{7,8},{8,9},{9,10},{10,1... | collective-permute-start | bytes 786440 | tf_op jit(solution)/shard_map/ppermute | solution.py:101
  170.8 31.5 %collective-permute-start.17 = (bf16[64,2048]{0,1:T(8,128)(2,1)}, bf16[64,2048]{0,1:T(8,128)(2,1)}, u32[]{:S(2)}, u32[]{:S(2)}) collective-permute-start(bf16[64,2048]{0,1:T(8,128)(2,1)} %collective-permute-done.16), channel_id=1, source_target_pairs={{0,15},{1,0},{2,1},{3,2},{4,3},{5,4},{6,5},{7,6},{8,7},{9,8},{10,9... | collective-permute-start | bytes 786440 | tf_op jit(solution)/shard_map/ppermute | solution.py:103
  179.0 57.4 %collective-permute-start.10 = (bf16[64,2048]{0,1:T(8,128)(2,1)}, bf16[64,2048]{0,1:T(8,128)(2,1)}, u32[]{:S(2)}, u32[]{:S(2)}) collective-permute-start(bf16[64,2048]{0,1:T(8,128)(2,1)} %collective-permute-done.9), channel_id=1, source_target_pairs={{0,1},{1,2},{2,3},{3,4},{4,5},{5,6},{6,7},{7,8},{8,9},{9,10},{10,1... | collective-permute-start | bytes 786440 | tf_op jit(solution)/shard_map/ppermute | solution.py:101
  182.1 122.2 %collective-permute-start.3 = (bf16[192,16,128]{2,0,1:T(8,128)(2,1)}, bf16[192,16,128]{2,0,1:T(8,128)(2,1)}, u32[]{:S(2)}, u32[]{:S(2)}) collective-permute-start(bf16[192,16,128]{2,0,1:T(8,128)(2,1)} %copy_bitcast_fusion), channel_id=1, source_target_pairs={{0,1},{1,2},{2,3},{3,4},{4,5},{5,6},{6,7},{7,8},{8,9},{9,10},{10,1... | collective-permute-start | bytes 2359304 | tf_op jit(solution)/shard_map/ppermute | solution.py:16
  202.3 45.4 %collective-permute-start.18 = (bf16[64,2048]{0,1:T(8,128)(2,1)}, bf16[64,2048]{0,1:T(8,128)(2,1)}, u32[]{:S(2)}, u32[]{:S(2)}) collective-permute-start(bf16[64,2048]{0,1:T(8,128)(2,1)} %collective-permute-done.17), channel_id=1, source_target_pairs={{0,15},{1,0},{2,1},{3,2},{4,3},{5,4},{6,5},{7,6},{8,7},{9,8},{10,9... | collective-permute-start | bytes 786440 | tf_op jit(solution)/shard_map/ppermute | solution.py:103
  236.4 17.1 %collective-permute-start.11 = (bf16[64,2048]{0,1:T(8,128)(2,1)}, bf16[64,2048]{0,1:T(8,128)(2,1)}, u32[]{:S(2)}, u32[]{:S(2)}) collective-permute-start(bf16[64,2048]{0,1:T(8,128)(2,1)} %collective-permute-done.10), channel_id=1, source_target_pairs={{0,1},{1,2},{2,3},{3,4},{4,5},{5,6},{6,7},{7,8},{8,9},{9,10},{10,1... | collective-permute-start | bytes 786440 | tf_op jit(solution)/shard_map/ppermute | solution.py:101
  236.4 17.1 %copy-start.6 = (bf16[64,2048]{0,1:T(8,128)(2,1)S(1)}, bf16[64,2048]{0,1:T(8,128)(2,1)}, u32[]{:S(2)}) copy-start(bf16[64,2048]{0,1:T(8,128)(2,1)} %copy-done.5) | copy-start | bytes 786436
  274.1 4.6 %copy-start.4 = (bf16[192,16,32]{2,0,1:T(8,128)(2,1)S(1)}, bf16[192,16,32]{2,0,1:T(8,128)(2,1)}, u32[]{:S(2)}) copy-start(bf16[192,16,32]{2,0,1:T(8,128)(2,1)} %get-tuple-element.20) | copy-start | bytes 589828
  282.0 4.6 %copy-start.2 = (f32[16,192,1024]{2,1,0:T(8,128)}, f32[16,192,1024]{2,1,0:T(8,128)S(1)}, u32[]{:S(2)}) copy-start(f32[16,192,1024]{2,1,0:T(8,128)S(1)} %get-tuple-element.31) | copy-start | bytes 37748740
  310.2 36.0 %copy-start.1 = (bf16[192,2048]{1,0:T(8,128)(2,1)S(1)}, bf16[192,2048]{1,0:T(8,128)(2,1)}, u32[]{:S(2)}) copy-start(bf16[192,2048]{1,0:T(8,128)(2,1)} %param.9) | copy-start | bytes 2359300
  (6 other events, 15.8 us)
Sparse Core Ops, SparseCore 0:
  10.1 161.1 all-gather.1
  320.8 25.3 reduce-scatter.1
